TPU v7x, 512 devices: a whole 4x8x8 slice. The times are simulated.
512 devices in a mesh: dp: 8 (over z_lo, core), basis: 64 (over z_hi, y, x).
Axes of the slice: x: 4, y: 8, z: 8 (z_hi: 2, z_lo: 4; z = z_hi * 4 + z_lo), core: 2. Of those that a mesh axis runs over, the one named last changes fastest.
Arguments:
- train_inputs: bfloat16 [8192, 8192], P('dp', 'basis'), may hold values from -6 to 6
- out_grads: bfloat16 [8192, 28672], P('dp', 'basis'), may hold values from -0.09375 to 0.09375
- basis_in: bfloat16 [8192, 128], P('basis'), may hold values from -0.0625 to 0.0625
- basis_out: bfloat16 [28672, 512], P('basis'), may hold values from -0.03125 to 0.03125
- query_left: bfloat16 [8192, 512], P('basis'), may hold values from -0.09375 to 0.09375
- query_right: bfloat16 [28672, 512], P('basis'), may hold values from -0.09375 to 0.09375
- eigenvalues: float32 [128, 512], P(None, 'basis'), may hold values from 0.2 to 4
Outputs:
- scores: float32 [8, 16], P('dp')
- damped_gradient: float32 [8, 128, 512], P('dp', None, 'basis')
All inputs are finite; a program needn't handle non-finite values.
Results may differ from a plain program's by a relative error of at most 0.003.
Values may be sent and summed in bfloat16 or wider, within the bound.
No kernel may reach another device: no remote copies, remote signals or barrier semaphores. Data moves between devices by JAX's collectives and lax.ppermute only.
A program may use at most 64 MiB of HBM per device.

v0:
```python
import jax
import jax.numpy as jnp
from jax import lax
from jax.sharding import PartitionSpec as P

Q = 16
R = 32


damping = 0.1


def on_device(train_inputs, out_grads, basis_in, basis_out, query_left, query_right, eigenvalues):
    width_in = basis_in.shape[1]
    left_part = jnp.einsum("ki,kr->ir", basis_in, query_left, preferred_element_type=jnp.float32)
    right_part = jnp.einsum("kr,kj->rj", query_right, basis_out, preferred_element_type=jnp.float32)
    proj_part = jnp.dot(train_inputs, basis_in, preferred_element_type=jnp.float32)
    proj_full, left_full = lax.psum((proj_part, left_part), "basis")
    proj_rows = proj_full.astype(jnp.bfloat16)
    moment = jnp.einsum("ti,tj->ij", proj_rows, out_grads, preferred_element_type=jnp.float32)
    rotated_part = jnp.dot(moment, basis_out.astype(jnp.float32), precision=lax.Precision.HIGHEST)
    rotated_mine, right_mine = (
        lax.psum_scatter(rotated_part, "basis", scatter_dimension=1, tiled=True),
        lax.psum_scatter(right_part, "basis", scatter_dimension=1, tiled=True),
    )
    damped = rotated_mine / (eigenvalues + damping)
    coupled = jnp.einsum("ij,rj->ir", damped, right_mine, precision=lax.Precision.HIGHEST)
    per_query = jnp.sum((left_full * coupled).reshape(width_in, Q, R), axis=(0, 2))
    scores = lax.psum(per_query, "basis")
    return (scores[None, :], damped[None])


def solution(mesh):
    in_specs = (
        P("dp", "basis"),
        P("dp", "basis"),
        P("basis", None),
        P("basis", None),
        P("basis", None),
        P("basis", None),
        P(None, "basis"),
    )
    out_specs = (P("dp", None), P("dp", None, "basis"))
    return jax.shard_map(
        on_device, mesh=mesh, in_specs=in_specs, out_specs=out_specs, check_vma=False
    )
```

profile of v0, /device:TPU:2, one launch (start us, length us, event | category | flops | bytes accessed | tf_op | source)
XLA Modules:
  0.0 1967.9 jit_solution(18410333367788438136)
XLA Ops:
  7.2 0.0 copy-start
  7.2 0.0 copy-start.4
  7.2 0.0 copy-start.3
  7.2 0.0 all-reduce.5.cloned.1.call-start
  7.2 1.9 fusion.5
  9.2 0.2 fusion.6
  9.4 438.5 %all-reduce.6 = bf16[1024,128]{1,0:T(8,128)(2,1)S(1)} all-reduce(f32[1024,128]{1,0:T(8,128)S(1)} %fusion.6), channel_id=1, replica_groups=mesh['dp'=8,'basis'=64] {'basis'}, use_global_device_ids=true, to_apply=%region_1.0 | all-reduce | flops 131072 | bytes 786432 | tf_op jit(solution)/shard_map/psum | solution.py:18
  447.8 0.0 copy-start.1
  447.9 0.4 fusion.8
  448.3 0.6 copy-done.1
  448.9 1.4 fusion.7
  450.3 0.0 all-reduce.5.cloned.1.call-update
  450.3 0.0 reduce-scatter.4.cloned.1.call-start
  450.4 0.9 copy-done.2
  451.3 1.5 convolution_bitcast_fusion
  452.8 0.0 reduce-scatter.4.cloned.1.call-update
  452.8 1.3 dynamic-slice
  454.7 840.0 %all-reduce.5.cloned.1.call-done = (f32[128,512]{1,0:T(8,128)}, f32[128,512]{0,1:T(8,128)}) async-done(((f32[128,512]{1,0:T(8,128)}, f32[128,512]{0,1:T(8,128)}), (f32[128,512]{1,0:T(8,128)}, f32[128,512]{0,1:T(8,128)})) %all-reduce.5.cloned.1.call-update) | async-done | bytes 524304 | tf_op jit(solution)/shard_map/psum | solution.py:18
  1294.8 1.3 fusion.4
  1296.1 438.7 %reduce-scatter.4.cloned.1.call-done = f32[8,512]{1,0:T(8,128)} async-done(((f32[512,512]{1,0:T(8,128)}), f32[8,512]{1,0:T(8,128)}) %reduce-scatter.4.cloned.1.call-update) | async-done | bytes 16400
  1734.7 1.4 fusion
  1736.1 0.1 reduce_sum.14
  1736.2 0.1 reduce_sum.18
  1736.3 224.7 %psum.23 = f32[1,16]{1,0:T(1,128)} all-reduce(f32[1,16]{1,0:T(1,128)S(1)} %bitcast.19), channel_id=1, replica_groups=mesh['dp'=8,'basis'=64] {'basis'}, use_global_device_ids=true, to_apply=%region_6.7 | all-reduce | flops 16 | bytes 128 | tf_op jit(solution)/shard_map/psum | solution.py:29
  (6 shorter events, 0.0 us)
Async XLA Ops:
  7.2 440.7 %copy-start = (bf16[1024,448]{0,1:T(8,128)(2,1)S(1)}, bf16[1024,448]{0,1:T(8,128)(2,1)}, u32[]{:S(2)}) copy-start(bf16[1024,448]{0,1:T(8,128)(2,1)} %param.8) | copy-start | bytes 2752516
  7.2 2.0 copy-start.4
  7.2 2.0 copy-start.3
  7.2 1287.6 %all-reduce.5.cloned.1.call-start = ((), (), s32[]{:S(2)}) async-start(), calls=%async_computation.2 | async-start | bytes 1048576 | tf_op jit(solution)/shard_map/psum | solution.py:18
  447.8 1.0 copy-start.1
  450.3 1.0 copy-start.2
  450.3 1284.4 %reduce-scatter.4.cloned.1.call-start = ((), (), s32[]{:S(2)}) async-start(), calls=%async_computation.1 | async-start | bytes 1064960
  454.1 840.7 %copy-start.5 = (f32[128,8]{0,1:T(8,128)S(1)}, f32[128,8]{0,1:T(8,128)}, u32[]{:S(2)}) copy-start(f32[128,8]{0,1:T(8,128)} %param.13) | copy-start | bytes 12292
Sparse Core Ops, SparseCore 0:
  450.4 844.2 all-reduce.4
  1297.6 437.1 reduce-scatter.3
where the time goes:
time: 1970 us
  waiting for transfers between devices  1280 us (65%)
  blocking collectives  663 us (34%)
    psum x1, waiting for transfers between devices, on_device(): proj_full, left_full = lax.psum((proj_part, left_part), 'basis')  840 us
    unnamed x3, waiting for transfers between devices  439 us
    psum x1, blocking collectives, on_device(): proj_full, left_full = lax.psum((proj_part, left_part), 'basis')  438 us
    psum x1, blocking collectives, on_device(): scores = lax.psum(per_query, 'basis')  225 us
  transfers between devices with their start and end apart: 2, of which 2 were waited for; matrix products, arithmetic and copies ran while one was open for 0% of the time, Pallas kernels for 0%

commit v1 on v0

v1 whole, which is shorter than its diff:
```python
import jax
import jax.numpy as jnp
from jax import lax
from jax.experimental import pallas as pl
from jax.experimental.pallas import tpu as pltpu
from jax.sharding import Mesh, PartitionSpec as P

F32 = jnp.float32
BF16 = jnp.bfloat16
damping = 0.1

PLANE = ("y", "x")
COLUMN = ("dp", "zh")
N = 32


def tn(a, b):
    return lax.dot_general(a, b, (((0,), (0,)), ((), ())), preferred_element_type=F32)


def call(kernel, out_shape, *args):
    return pl.pallas_call(
        kernel,
        out_shape=out_shape,
        compiler_params=pltpu.CompilerParams(vmem_limit_bytes=12 * 1024 * 1024),
    )(*args)


def partials(x_ref, bi_ref, ql_ref, bo_ref, qr_ref, o_ref):
    dp = lax.axis_index("dp")
    block = pl.ds(pl.multiple_of((dp // 2) * 128, 128), 128)
    half = pl.ds(pl.multiple_of((dp % 2) * 256, 128), 256)
    proj = jnp.dot(x_ref[...], bi_ref[...], preferred_element_type=F32)
    o_ref[:, 0:32, :] = proj.reshape(N, 32, 128)
    right = tn(bo_ref[:, half], qr_ref[:, block])
    o_ref[:, 32:40, :] = right.reshape(N, 8, 128)
    left = tn(ql_ref[:, block], bi_ref[...]).reshape(N // 2, 1, 8, 128)
    o_ref[:, 40:48, :] = jnp.broadcast_to(left, (N // 2, 2, 8, 128)).reshape(N, 8, 128)


def plane_sum(r_ref, eig_ref, o_ref):
    o_ref[0:48] = jnp.sum(r_ref[...], axis=0)
    o_ref[48:56] = eig_ref[...]


def finish(a_ref, b_ref, o_ref, right_ref, eig_ref):
    total = a_ref[0:48] + b_ref[0:48]
    left = total[40:48]
    high = left.astype(BF16).astype(F32)
    odd = lax.axis_index("x") % 2 == 1
    piece = jnp.where(odd, left - high, high).astype(BF16)
    o_ref[:, 0:32, :] = jnp.broadcast_to(total[0:32].astype(BF16)[None], (N, 32, 128))
    o_ref[:, 32:40, :] = jnp.broadcast_to(piece[None], (N, 8, 128))
    right_ref[...] = total[32:40]
    first = lax.axis_index("zh") == 0
    eig_ref[0:8] = jnp.where(first, a_ref[48:56], b_ref[48:56])
    eig_ref[8:16] = jnp.where(first, b_ref[48:56], a_ref[48:56])


def rotate(r_ref, g_ref, bo_ref, right_ref, o_ref, w_ref):
    proj = r_ref[:, 0:32, :].reshape(N * 32, 128)
    moment = jnp.dot(g_ref[...], proj, preferred_element_type=F32)
    m1 = moment.astype(BF16)
    rest = moment - m1.astype(F32)
    m2 = rest.astype(BF16)
    m3 = (rest - m2.astype(F32)).astype(BF16)
    bo = bo_ref[...]
    rotated = (tn(bo, m3) + tn(bo, m2)) + tn(bo, m1)
    o_ref[:, 0:8, :] = rotated[0:256].reshape(N, 8, 128)
    o_ref[:, 8:16, :] = rotated[256:512].reshape(N, 8, 128)
    pieces = r_ref[:, 32:40, :].astype(F32).reshape(N // 2, 2, 8, 128)
    left = (pieces[:, 0] + pieces[:, 1]).reshape(128, 128)
    right = right_ref[...]
    rows = jnp.concatenate([right, right, right, right], axis=0)
    query = lax.broadcasted_iota(jnp.int32, (32, 128), 0) // 8
    column = lax.broadcasted_iota(jnp.int32, (32, 128), 1) // 32
    rows = jnp.where(query == column, rows, 0.0)
    w_ref[...] = jnp.dot(rows, left, precision=lax.Precision.HIGHEST, preferred_element_type=F32)


def column_pack(r_ref, w_ref, o_ref, s_ref):
    total = jnp.sum(r_ref[...], axis=0)
    zh = lax.axis_index("zh")
    mine = w_ref[pl.ds(pl.multiple_of(zh * 16, 16), 16)]
    o_ref[...] = jnp.broadcast_to(mine[None], (16, 16, 128))
    o_ref[2 * lax.axis_index("dp") + 1 - zh] = total
    s_ref[...] = total


def score(r_ref, s_ref, w_ref, eig_ref, d_ref, o_ref):
    zh = lax.axis_index("zh")
    partner = 2 * lax.axis_index("dp") + 1 - zh
    damped = (s_ref[...] + r_ref[partner]) / (eig_ref[...] + damping)
    d_ref[...] = jnp.where(zh == 0, damped[0:8], damped[8:16])
    local = w_ref[pl.ds(pl.multiple_of((1 - zh) * 16, 16), 16)]

    def weights(source, rows):
        return jnp.where(partner == source, local[rows], r_ref[source, rows])

    sums = []
    for q in range(16):
        rows = slice((q % 2) * 8, (q % 2) * 8 + 8)
        even = 4 * (q // 4) + (q % 4) // 2
        part = weights(even, rows) * damped[0:8] + weights(even + 2, rows) * damped[8:16]
        sums.append(jnp.sum(part, axis=0, keepdims=True))
    sums = jnp.concatenate(sums, axis=0)
    ones = jnp.ones((8, 128), F32)
    row = lax.dot_general(ones, jnp.concatenate([sums, jnp.zeros((112, 128), F32)], axis=0),
                          (((1,), (1,)), ((), ())), precision=lax.Precision.HIGHEST, preferred_element_type=F32)
    o_ref[...] = jnp.broadcast_to(row[None], (N, 8, 128))


def last_sum(r_ref, o_ref):
    o_ref[...] = jnp.sum(r_ref[...], axis=0)[0:1, 0:16]


def on_device(train_inputs, out_grads, basis_in, basis_out, query_left, query_right, eigenvalues):
    def shape(*dims, dtype=F32):
        return jax.ShapeDtypeStruct(dims, dtype)

    part = call(partials, shape(N, 48, 128), train_inputs, basis_in, query_left, basis_out, query_right)
    part = lax.all_to_all(part, PLANE, 0, 0, tiled=True)
    mine = call(plane_sum, shape(56, 128), part, eigenvalues.T)
    other = lax.ppermute(mine, "zh", [(0, 1), (1, 0)])
    full, right, eig = call(
        finish, (shape(N, 40, 128, dtype=BF16), shape(8, 128), shape(16, 128)), mine, other)
    full = lax.all_to_all(full, PLANE, 0, 0, tiled=True)
    rotated, weights = call(
        rotate, (shape(N, 16, 128), shape(32, 128)), full, out_grads.T, basis_out, right)
    rotated = lax.all_to_all(rotated, PLANE, 0, 0, tiled=True)
    packed, half = call(column_pack, (shape(16, 16, 128), shape(16, 128)), rotated, weights)
    packed = lax.all_to_all(packed, COLUMN, 0, 0, tiled=True)
    damped, scores = call(score, (shape(8, 128), shape(N, 8, 128)), packed, half, weights, eig)
    scores = lax.all_to_all(scores, PLANE, 0, 0, tiled=True)
    scores = call(last_sum, shape(1, 16), scores)
    return scores, damped.T[None]


def solution(mesh):
    fine = Mesh(mesh.devices.reshape(8, 2, 8, 4), ("dp", "zh", "y", "x"))
    basis = ("zh", "y", "x")
    in_specs = (
        P("dp", basis),
        P("dp", basis),
        P(basis, None),
        P(basis, None),
        P(basis, None),
        P(basis, None),
        P(None, basis),
    )
    out_specs = (P("dp", None), P("dp", None, basis))
    return jax.shard_map(
        on_device, mesh=fine, in_specs=in_specs, out_specs=out_specs, check_vma=False
    )
```

time: 1970 us -> 117 us (0.06)
  the two profiles are of different devices: /device:TPU:2 before, /device:TPU:1 now
where the time goes in v1:
time: 117 us
  blocking collectives  96.2 us (82%)
  starting transfers between devices  10.8 us (9%)
  local copies, waits for them, and re-layouts  4.66 us (4%)
  Pallas kernels  3.02 us (3%)
  waiting for transfers between devices  1.27 us (1%)
    all_to_all x1, blocking collectives, on_device(): part = lax.all_to_all(part, PLANE, 0, 0, tiled=True)  31.4 us
    all_to_all x1, blocking collectives, on_device(): packed = lax.all_to_all(packed, COLUMN, 0, 0, tiled=True)  21 us
    all_to_all x1, blocking collectives, on_device(): full = lax.all_to_all(full, PLANE, 0, 0, tiled=True)  16.4 us
    all_to_all x1, blocking collectives, on_device(): rotated = lax.all_to_all(rotated, PLANE, 0, 0, tiled=True)  14.5 us
    all_to_all x1, blocking collectives, on_device(): scores = lax.all_to_all(scores, PLANE, 0, 0, tiled=True)  12.9 us
    ppermute x1, starting transfers between devices, on_device(): other = lax.ppermute(mine, 'zh', [(0, 1), (1, 0)])  10.8 us
    unnamed x16, local copies, waits for them, and re-layouts  4.66 us
    pallas_call x7, Pallas kernels, call(): pl.pallas_call(kernel, out_shape=out_shape, compiler_params=pltpu.Compile...  3.02 us
  transfers between devices with their start and end apart: 1, of which 1 were waited for; matrix products, arithmetic and copies ran while one was open for 0% of the time, Pallas kernels for 0%

profile of v1, /device:TPU:1, one launch (start us, length us, event | category | flops | bytes accessed | tf_op | source)
XLA Modules:
  0.0 116.6 jit_solution(153382364298236442)
XLA Ops:
  0.6 0.0 copy-start
  0.6 1.0 copy-done
  1.7 0.0 copy-start.3
  1.7 1.0 copy-done.3
  2.7 0.9 copy-done.4
  3.6 0.9 copy-done.5
  4.5 0.8 copy-done.6
  5.3 0.3 shard_map.86
  5.6 0.0 copy-start.7
  5.6 31.4 %all_to_all.25.r_ref = f32[32,48,128]{2,1,0:T(8,128)S(1)} all-to-all(f32[32,48,128]{2,1,0:T(8,128)S(1)} %shard_map.86), channel_id=1, replica_groups=mesh['dp'=8,'zh'=2,'y'=8,'x'=4] {'y','x'}, dimensions={0} | all-to-all | bytes 1572864 | tf_op jit(solution)/shard_map/all_to_all | solution.py:122
  37.0 0.0 copy-done.7
  37.0 0.1 shard_map.87.a_ref
  37.1 0.0 copy-start.1
  37.1 10.8 %collective-permute-start = (f32[56,128]{1,0:T(8,128)S(1)}, f32[56,128]{1,0:T(8,128)S(1)}, u32[]{:S(2)}, u32[]{:S(2)}) collective-permute-start(f32[56,128]{1,0:T(8,128)S(1)} %shard_map.87.a_ref), channel_id=1, source_target_pairs={{0,32},{32,0},{1,33},{33,1},{2,34},{34,2},{3,35},{35,3},{4,36},{36... | collective-permute-start | bytes 86024 | tf_op jit(solution)/shard_map/ppermute | solution.py:124
  47.8 1.3 %collective-permute-done.b_ref = f32[56,128]{1,0:T(8,128)S(1)} collective-permute-done((f32[56,128]{1,0:T(8,128)S(1)}, f32[56,128]{1,0:T(8,128)S(1)}, u32[]{:S(2)}, u32[]{:S(2)}) %collective-permute-start) | collective-permute-done | bytes 28704 | tf_op jit(solution)/shard_map/ppermute | solution.py:124
  49.2 16.4 %all_to_all.26.r_ref = bf16[32,40,128]{2,1,0:T(8,128)(2,1)S(1)} all-to-all(bf16[32,40,128]{2,1,0:T(8,128)(2,1)S(1)} %get-tuple-element.11), channel_id=1, replica_groups=mesh['dp'=8,'zh'=2,'y'=8,'x'=4] {'y','x'}, dimensions={0} | all-to-all | bytes 655360 | tf_op jit(solution)/shard_map/all_to_all | solution.py:127
  65.6 0.0 copy-done.2
  65.6 0.0 copy-done.1
  65.6 1.4 %shard_map.89 = (f32[32,16,128]{2,1,0:T(8,128)S(1)}, f32[32,128]{1,0:T(8,128)S(1)}) custom-call(bf16[32,40,128]{2,1,0:T(8,128)(2,1)S(1)} %all_to_all.26.r_ref, bf16[448,1024]{1,0:T(8,128)(2,1)S(1)} %bitcast.5, bf16[448,512]{1,0:T(8,128)(2,1)S(1)} %copy-done.1, f32[8,128]{1,0:T(8,128)S(1)} %get-tuple-element.12.right_ref), custom_call_target="tpu_custom_call" | custom-call | tf_op jit(solution)/shard_map/pallas_call | solution.py:22
  66.9 14.5 %all_to_all.27.r_ref = f32[32,16,128]{2,1,0:T(8,128)S(1)} all-to-all(f32[32,16,128]{2,1,0:T(8,128)S(1)} %get-tuple-element.13), channel_id=1, replica_groups=mesh['dp'=8,'zh'=2,'y'=8,'x'=4] {'y','x'}, dimensions={0} | all-to-all | bytes 524288 | tf_op jit(solution)/shard_map/all_to_all | solution.py:130
  81.5 21.0 %all_to_all.28.r_ref = f32[16,16,128]{2,1,0:T(8,128)S(1)} all-to-all(f32[16,16,128]{2,1,0:T(8,128)S(1)} %get-tuple-element.15), channel_id=1, replica_groups=mesh['dp'=8,'zh'=2,'y'=8,'x'=4] {'dp','zh'}, dimensions={0} | all-to-all | bytes 262144 | tf_op jit(solution)/shard_map/all_to_all | solution.py:132
  102.5 0.6 shard_map.91
  103.2 12.9 %all_to_all.29.r_ref = f32[32,8,128]{2,1,0:T(8,128)S(1)} all-to-all(f32[32,8,128]{2,1,0:T(8,128)S(1)} %get-tuple-element.18), channel_id=1, replica_groups=mesh['dp'=8,'zh'=2,'y'=8,'x'=4] {'y','x'}, dimensions={0} | all-to-all | bytes 262144 | tf_op jit(solution)/shard_map/all_to_all | solution.py:134
  116.1 0.5 shard_map.92
  (6 shorter events, 0.1 us)
Async XLA Ops:
  0.6 1.0 copy-start
  1.7 1.0 copy-start.3
  2.7 0.9 copy-start.4
  3.6 0.9 copy-start.5
  4.5 0.8 copy-start.6
  5.6 31.4 %copy-start.7 = (f32[128,8]{0,1:T(8,128)S(1)}, f32[128,8]{0,1:T(8,128)}, u32[]{:S(2)}) copy-start(f32[128,8]{0,1:T(8,128)} %param.13) | copy-start | bytes 12292
  37.0 28.6 %copy-start.2 = (bf16[1024,448]{0,1:T(8,128)(2,1)S(1)}, bf16[1024,448]{0,1:T(8,128)(2,1)}, u32[]{:S(2)}) copy-start(bf16[1024,448]{0,1:T(8,128)(2,1)} %param.8) | copy-start | bytes 2752516
  37.1 28.5 %copy-start.1 = (bf16[448,512]{1,0:T(8,128)(2,1)S(1)}, bf16[448,512]{1,0:T(8,128)(2,1)}, u32[]{:S(2)}) copy-start(bf16[448,512]{1,0:T(8,128)(2,1)} %bo_ref.3) | copy-start | bytes 1376260
  37.1 12.0 %collective-permute-start = (f32[56,128]{1,0:T(8,128)S(1)}, f32[56,128]{1,0:T(8,128)S(1)}, u32[]{:S(2)}, u32[]{:S(2)}) collective-permute-start(f32[56,128]{1,0:T(8,128)S(1)} %shard_map.87.a_ref), channel_id=1, source_target_pairs={{0,32},{32,0},{1,33},{33,1},{2,34},{34,2},{3,35},{35,3},{4,36},{36... | collective-permute-start | bytes 86024 | tf_op jit(solution)/shard_map/ppermute | solution.py:124

commit v2 on v1

--- a/solution.py
+++ b/solution.py
@@ -26,31 +26,55 @@
     )(*args)
 
 
-def partials(x_ref, bi_ref, ql_ref, bo_ref, qr_ref, o_ref):
+def split(value):
+    high = value.astype(BF16).astype(F32)
+    return high, value - high
+
+
+def partials(x_hbm, bi_hbm, ql_hbm, bo_hbm, qr_hbm, o_ref, x_ref, bi_ref, ql_ref, bo_ref, qr_ref, sem):
     dp = lax.axis_index("dp")
     block = pl.ds(pl.multiple_of((dp // 2) * 128, 128), 128)
     half = pl.ds(pl.multiple_of((dp % 2) * 256, 128), 256)
+    moves = [
+        (bi_hbm, bi_ref), (x_hbm, x_ref), (ql_hbm.at[:, block], ql_ref),
+        (qr_hbm.at[:, block], qr_ref), (bo_hbm.at[:, half], bo_ref),
+    ]
+    moves = [pltpu.make_async_copy(src, dst, sem.at[k]) for k, (src, dst) in enumerate(moves)]
+    for move in moves:
+        move.start()
+    moves[0].wait()
+    moves[1].wait()
     proj = jnp.dot(x_ref[...], bi_ref[...], preferred_element_type=F32)
-    o_ref[:, 0:32, :] = proj.reshape(N, 32, 128)
-    right = tn(bo_ref[:, half], qr_ref[:, block])
-    o_ref[:, 32:40, :] = right.reshape(N, 8, 128)
-    left = tn(ql_ref[:, block], bi_ref[...]).reshape(N // 2, 1, 8, 128)
-    o_ref[:, 40:48, :] = jnp.broadcast_to(left, (N // 2, 2, 8, 128)).reshape(N, 8, 128)
+    high, low = split(proj)
+    o_ref[:, 0:32, :] = high.astype(BF16).reshape(N, 32, 128)
+    o_ref[:, 32:64, :] = low.astype(BF16).reshape(N, 32, 128)
+    moves[2].wait()
+    high, low = split(tn(ql_ref[...], bi_ref[...]).reshape(N // 2, 8, 128))
+    top = lax.broadcasted_iota(jnp.int32, (N // 2, 8, 128), 1) < 4
+    even = jnp.where(top, high, jnp.roll(low, 4, axis=1))
+    odd = jnp.where(top, jnp.roll(high, 4, axis=1), low)
+    left = jnp.concatenate([even[:, None], odd[:, None]], axis=1).reshape(N, 8, 128)
+    moves[3].wait()
+    moves[4].wait()
+    high, low = split(tn(bo_ref[...], qr_ref[...]).reshape(N, 8, 128))
+    o_ref[:, 64:88, :] = jnp.concatenate([high, low, left], axis=1).astype(BF16)
 
 
 def plane_sum(r_ref, eig_ref, o_ref):
-    o_ref[0:48] = jnp.sum(r_ref[...], axis=0)
+    total = jnp.sum(r_ref[...].astype(F32), axis=0)
+    o_ref[0:32] = total[0:32] + total[32:64]
+    o_ref[32:40] = total[64:72] + total[72:80]
+    o_ref[40:48] = total[80:88]
     o_ref[48:56] = eig_ref[...]
 
 
 def finish(a_ref, b_ref, o_ref, right_ref, eig_ref):
     total = a_ref[0:48] + b_ref[0:48]
-    left = total[40:48]
-    high = left.astype(BF16).astype(F32)
-    odd = lax.axis_index("x") % 2 == 1
-    piece = jnp.where(odd, left - high, high).astype(BF16)
-    o_ref[:, 0:32, :] = jnp.broadcast_to(total[0:32].astype(BF16)[None], (N, 32, 128))
-    o_ref[:, 32:40, :] = jnp.broadcast_to(piece[None], (N, 8, 128))
+    left = total[40:48] + jnp.roll(total[40:48], 4, axis=0)
+    high, low = split(left)
+    piece = jnp.where(lax.broadcasted_iota(jnp.int32, (8, 128), 0) < 4, high, low)
+    rows = jnp.concatenate([total[0:32], piece], axis=0).astype(BF16)
+    o_ref[...] = jnp.broadcast_to(rows[None], (N, 40, 128))
     right_ref[...] = total[32:40]
     first = lax.axis_index("zh") == 0
     eig_ref[0:8] = jnp.where(first, a_ref[48:56], b_ref[48:56])
@@ -60,16 +84,16 @@
 def rotate(r_ref, g_ref, bo_ref, right_ref, o_ref, w_ref):
     proj = r_ref[:, 0:32, :].reshape(N * 32, 128)
     moment = jnp.dot(g_ref[...], proj, preferred_element_type=F32)
-    m1 = moment.astype(BF16)
-    rest = moment - m1.astype(F32)
-    m2 = rest.astype(BF16)
-    m3 = (rest - m2.astype(F32)).astype(BF16)
-    bo = bo_ref[...]
-    rotated = (tn(bo, m3) + tn(bo, m2)) + tn(bo, m1)
+    m1, rest = split(moment)
+    m2, m3 = split(rest)
+    rotated = tn(bo_ref[...], jnp.concatenate([m1, m2, m3], axis=1).astype(BF16))
+    rotated = (rotated[:, 256:384] + rotated[:, 128:256]) + rotated[:, 0:128]
     o_ref[:, 0:8, :] = rotated[0:256].reshape(N, 8, 128)
     o_ref[:, 8:16, :] = rotated[256:512].reshape(N, 8, 128)
-    pieces = r_ref[:, 32:40, :].astype(F32).reshape(N // 2, 2, 8, 128)
-    left = (pieces[:, 0] + pieces[:, 1]).reshape(128, 128)
+    pieces = r_ref[:, 32:40, :].astype(F32)
+    pieces = (pieces + jnp.roll(pieces, 4, axis=1)).reshape(N // 2, 2, 8, 128)
+    top = lax.broadcasted_iota(jnp.int32, (N // 2, 8, 128), 1) < 4
+    left = jnp.where(top, pieces[:, 0], pieces[:, 1]).reshape(128, 128)
     right = right_ref[...]
     rows = jnp.concatenate([right, right, right, right], axis=0)
     query = lax.broadcasted_iota(jnp.int32, (32, 128), 0) // 8
@@ -107,18 +131,32 @@
     ones = jnp.ones((8, 128), F32)
     row = lax.dot_general(ones, jnp.concatenate([sums, jnp.zeros((112, 128), F32)], axis=0),
                           (((1,), (1,)), ((), ())), precision=lax.Precision.HIGHEST, preferred_element_type=F32)
-    o_ref[...] = jnp.broadcast_to(row[None], (N, 8, 128))
+    o_ref[...] = jnp.broadcast_to(row[None, 0:1], (N, 1, 128))
 
 
 def last_sum(r_ref, o_ref):
-    o_ref[...] = jnp.sum(r_ref[...], axis=0)[0:1, 0:16]
+    o_ref[...] = jnp.sum(r_ref[...], axis=0)[:, 0:16]
 
 
 def on_device(train_inputs, out_grads, basis_in, basis_out, query_left, query_right, eigenvalues):
     def shape(*dims, dtype=F32):
         return jax.ShapeDtypeStruct(dims, dtype)
 
-    part = call(partials, shape(N, 48, 128), train_inputs, basis_in, query_left, basis_out, query_right)
+    hbm = pl.BlockSpec(memory_space=pltpu.HBM)
+    part = pl.pallas_call(
+        partials,
+        out_shape=shape(N, 88, 128, dtype=BF16),
+        in_specs=[hbm] * 5,
+        scratch_shapes=[
+            pltpu.VMEM((1024, 128), BF16),
+            pltpu.VMEM((128, 128), BF16),
+            pltpu.VMEM((128, 128), BF16),
+            pltpu.VMEM((448, 256), BF16),
+            pltpu.VMEM((448, 128), BF16),
+            pltpu.SemaphoreType.DMA((5,)),
+        ],
+        compiler_params=pltpu.CompilerParams(vmem_limit_bytes=12 * 1024 * 1024),
+    )(*(pltpu.with_memory_space_constraint(v, pltpu.HBM) for v in (train_inputs, basis_in, query_left, basis_out, query_right)))
     part = lax.all_to_all(part, PLANE, 0, 0, tiled=True)
     mine = call(plane_sum, shape(56, 128), part, eigenvalues.T)
     other = lax.ppermute(mine, "zh", [(0, 1), (1, 0)])
@@ -130,7 +168,7 @@
     rotated = lax.all_to_all(rotated, PLANE, 0, 0, tiled=True)
     packed, half = call(column_pack, (shape(16, 16, 128), shape(16, 128)), rotated, weights)
     packed = lax.all_to_all(packed, COLUMN, 0, 0, tiled=True)
-    damped, scores = call(score, (shape(8, 128), shape(N, 8, 128)), packed, half, weights, eig)
+    damped, scores = call(score, (shape(8, 128), shape(N, 1, 128)), packed, half, weights, eig)
     scores = lax.all_to_all(scores, PLANE, 0, 0, tiled=True)
     scores = call(last_sum, shape(1, 16), scores)
     return scores, damped.T[None]

time: 117 us -> 112 us (0.957)
  local copies, waits for them, and re-layouts: 4.66 us -> 0.02 us
  blocking collectives: 96.2 us -> 94.1 us
  Pallas kernels: 3.02 us -> 4.39 us
    unnamed x16 -> x6, local copies, waits for them, and re-layouts: 4.66 us -> 0.02 us
    pallas_call x0 -> x1, Pallas kernels: none -> 1.79 us  [on_device(): pl.pallas_call(partials, out_shape=shape(N, 88, 128, dtype=BF16), in_spec...]
    pallas_call x7 -> x6, Pallas kernels: 3.02 us -> 2.6 us  [call(): pl.pallas_call(kernel, out_shape=out_shape, compiler_params=pltpu.Compile...]
where the time goes in v2:
time: 112 us; the launch traced here: 111 us
  blocking collectives  94.1 us (84%)
  starting transfers between devices  10.8 us (10%)
  Pallas kernels  4.39 us (4%)
  waiting for transfers between devices  1.27 us (1%)
    all_to_all x1, blocking collectives, on_device(): part = lax.all_to_all(part, PLANE, 0, 0, tiled=True)  30.3 us
    all_to_all x1, blocking collectives, on_device(): packed = lax.all_to_all(packed, COLUMN, 0, 0, tiled=True)  21.2 us
    all_to_all x1, blocking collectives, on_device(): full = lax.all_to_all(full, PLANE, 0, 0, tiled=True)  16.1 us
    all_to_all x1, blocking collectives, on_device(): rotated = lax.all_to_all(rotated, PLANE, 0, 0, tiled=True)  14.3 us
    all_to_all x1, blocking collectives, on_device(): scores = lax.all_to_all(scores, PLANE, 0, 0, tiled=True)  12.1 us
    ppermute x1, starting transfers between devices, on_device(): other = lax.ppermute(mine, 'zh', [(0, 1), (1, 0)])  10.8 us
    pallas_call x6, Pallas kernels, call(): pl.pallas_call(kernel, out_shape=out_shape, compiler_params=pltpu.Compile...  2.6 us
  transfers between devices with their start and end apart: 1, of which 1 were waited for; matrix products, arithmetic and copies ran while one was open for 0% of the time, Pallas kernels for 0%

profile of v2, /device:TPU:1, one launch (start us, length us, event | category | flops | bytes accessed | tf_op | source)
XLA Modules:
  0.0 111.2 jit_solution(8898870862938280999)
XLA Ops:
  0.6 1.8 %shard_map.86 = bf16[32,88,128]{2,1,0:T(8,128)(2,1)S(1)} custom-call(bf16[1024,128]{1,0:T(8,128)(2,1)} %x_hbm.1, bf16[128,128]{1,0:T(8,128)(2,1)} %bi_hbm.1, bf16[128,512]{1,0:T(8,128)(2,1)} %ql_hbm.1, bf16[448,512]{1,0:T(8,128)(2,1)} %bo_ref.1, bf16[448,512]{1,0:T(8,128)(2,1)} %qr_hbm.1), custom_call_target="tpu_custom_call" | custom-call | tf_op jit(solution)/shard_map/pallas_call | solution.py:146
  2.4 0.0 copy-start.2
  2.4 30.3 %all_to_all.25.r_ref = bf16[32,88,128]{2,1,0:T(8,128)(2,1)S(1)} all-to-all(bf16[32,88,128]{2,1,0:T(8,128)(2,1)S(1)} %shard_map.86), channel_id=1, replica_groups=mesh['dp'=8,'zh'=2,'y'=8,'x'=4] {'y','x'}, dimensions={0} | all-to-all | bytes 1441792 | tf_op jit(solution)/shard_map/all_to_all | solution.py:160
  32.7 0.0 copy-start.1
  32.7 0.0 copy-done.2
  32.7 0.1 shard_map.87.a_ref
  32.8 0.0 copy-start
  32.9 10.8 %collective-permute-start = (f32[56,128]{1,0:T(8,128)S(1)}, f32[56,128]{1,0:T(8,128)S(1)}, u32[]{:S(2)}, u32[]{:S(2)}) collective-permute-start(f32[56,128]{1,0:T(8,128)S(1)} %shard_map.87.a_ref), channel_id=1, source_target_pairs={{0,32},{32,0},{1,33},{33,1},{2,34},{34,2},{3,35},{35,3},{4,36},{36... | collective-permute-start | bytes 86024 | tf_op jit(solution)/shard_map/ppermute | solution.py:162
  43.6 1.3 %collective-permute-done.b_ref = f32[56,128]{1,0:T(8,128)S(1)} collective-permute-done((f32[56,128]{1,0:T(8,128)S(1)}, f32[56,128]{1,0:T(8,128)S(1)}, u32[]{:S(2)}, u32[]{:S(2)}) %collective-permute-start) | collective-permute-done | bytes 28704 | tf_op jit(solution)/shard_map/ppermute | solution.py:162
  44.9 16.1 %all_to_all.26.r_ref = bf16[32,40,128]{2,1,0:T(8,128)(2,1)S(1)} all-to-all(bf16[32,40,128]{2,1,0:T(8,128)(2,1)S(1)} %get-tuple-element.11), channel_id=1, replica_groups=mesh['dp'=8,'zh'=2,'y'=8,'x'=4] {'y','x'}, dimensions={0} | all-to-all | bytes 655360 | tf_op jit(solution)/shard_map/all_to_all | solution.py:165
  61.1 0.0 copy-done.1
  61.1 0.0 copy-done
  61.1 1.2 %shard_map.89 = (f32[32,16,128]{2,1,0:T(8,128)S(1)}, f32[32,128]{1,0:T(8,128)S(1)}) custom-call(bf16[32,40,128]{2,1,0:T(8,128)(2,1)S(1)} %all_to_all.26.r_ref, bf16[448,1024]{1,0:T(8,128)(2,1)S(1)} %bitcast.5, bf16[448,512]{1,0:T(8,128)(2,1)S(1)} %copy-done, f32[8,128]{1,0:T(8,128)S(1)} %get-tuple-element.12.right_ref), custom_call_target="tpu_custom_call" | custom-call | tf_op jit(solution)/shard_map/pallas_call | solution.py:22
  62.3 14.3 %all_to_all.27.r_ref = f32[32,16,128]{2,1,0:T(8,128)S(1)} all-to-all(f32[32,16,128]{2,1,0:T(8,128)S(1)} %get-tuple-element.13), channel_id=1, replica_groups=mesh['dp'=8,'zh'=2,'y'=8,'x'=4] {'y','x'}, dimensions={0} | all-to-all | bytes 524288 | tf_op jit(solution)/shard_map/all_to_all | solution.py:168
  76.7 21.2 %all_to_all.28.r_ref = f32[16,16,128]{2,1,0:T(8,128)S(1)} all-to-all(f32[16,16,128]{2,1,0:T(8,128)S(1)} %get-tuple-element.15), channel_id=1, replica_groups=mesh['dp'=8,'zh'=2,'y'=8,'x'=4] {'dp','zh'}, dimensions={0} | all-to-all | bytes 262144 | tf_op jit(solution)/shard_map/all_to_all | solution.py:170
  97.9 0.6 shard_map.91
  98.5 12.1 %all_to_all.29.r_ref = f32[32,1,128]{2,1,0:T(1,128)S(1)} all-to-all(f32[32,1,128]{2,1,0:T(1,128)S(1)} %get-tuple-element.18), channel_id=1, replica_groups=mesh['dp'=8,'zh'=2,'y'=8,'x'=4] {'y','x'}, dimensions={0} | all-to-all | bytes 32768 | tf_op jit(solution)/shard_map/all_to_all | solution.py:172
  110.6 0.5 shard_map.92
  (2 shorter events, 0.1 us)
Async XLA Ops:
  2.4 30.3 %copy-start.2 = (f32[128,8]{0,1:T(8,128)S(1)}, f32[128,8]{0,1:T(8,128)}, u32[]{:S(2)}) copy-start(f32[128,8]{0,1:T(8,128)} %param.13) | copy-start | bytes 12292
  32.7 28.3 %copy-start.1 = (bf16[1024,448]{0,1:T(8,128)(2,1)S(1)}, bf16[1024,448]{0,1:T(8,128)(2,1)}, u32[]{:S(2)}) copy-start(bf16[1024,448]{0,1:T(8,128)(2,1)} %param.8) | copy-start | bytes 2752516
  32.8 28.2 %copy-start = (bf16[448,512]{1,0:T(8,128)(2,1)S(1)}, bf16[448,512]{1,0:T(8,128)(2,1)}, u32[]{:S(2)}) copy-start(bf16[448,512]{1,0:T(8,128)(2,1)} %bo_ref.1) | copy-start | bytes 1376260
  32.9 12.0 %collective-permute-start = (f32[56,128]{1,0:T(8,128)S(1)}, f32[56,128]{1,0:T(8,128)S(1)}, u32[]{:S(2)}, u32[]{:S(2)}) collective-permute-start(f32[56,128]{1,0:T(8,128)S(1)} %shard_map.87.a_ref), channel_id=1, source_target_pairs={{0,32},{32,0},{1,33},{33,1},{2,34},{34,2},{3,35},{35,3},{4,36},{36... | collective-permute-start | bytes 86024 | tf_op jit(solution)/shard_map/ppermute | solution.py:162

commit v3 on v2

--- a/solution.py
+++ b/solution.py
@@ -134,8 +134,9 @@
     o_ref[...] = jnp.broadcast_to(row[None, 0:1], (N, 1, 128))
 
 
-def last_sum(r_ref, o_ref):
+def last_sum(r_ref, d_ref, o_ref, e_ref):
     o_ref[...] = jnp.sum(r_ref[...], axis=0)[:, 0:16]
+    e_ref[...] = d_ref[...]
 
 
 def on_device(train_inputs, out_grads, basis_in, basis_out, query_left, query_right, eigenvalues):
@@ -170,7 +171,7 @@
     packed = lax.all_to_all(packed, COLUMN, 0, 0, tiled=True)
     damped, scores = call(score, (shape(8, 128), shape(N, 1, 128)), packed, half, weights, eig)
     scores = lax.all_to_all(scores, PLANE, 0, 0, tiled=True)
-    scores = call(last_sum, shape(1, 16), scores)
+    scores, damped = call(last_sum, (shape(1, 16), shape(8, 128)), scores, damped)
     return scores, damped.T[None]
 
 

time: 112 us -> 111 us (level)
  no operation moved by 1% of the time
where the time goes in v3:
time: 111 us
  blocking collectives  94.1 us (85%)
  starting transfers between devices  10.8 us (10%)
  Pallas kernels  3.97 us (4%)
  waiting for transfers between devices  1.27 us (1%)
    all_to_all x1, blocking collectives, on_device(): part = lax.all_to_all(part, PLANE, 0, 0, tiled=True)  30.3 us
    all_to_all x1, blocking collectives, on_device(): packed = lax.all_to_all(packed, COLUMN, 0, 0, tiled=True)  21.2 us
    all_to_all x1, blocking collectives, on_device(): full = lax.all_to_all(full, PLANE, 0, 0, tiled=True)  16.1 us
    all_to_all x1, blocking collectives, on_device(): rotated = lax.all_to_all(rotated, PLANE, 0, 0, tiled=True)  14.3 us
    all_to_all x1, blocking collectives, on_device(): scores = lax.all_to_all(scores, PLANE, 0, 0, tiled=True)  12.1 us
    ppermute x1, starting transfers between devices, on_device(): other = lax.ppermute(mine, 'zh', [(0, 1), (1, 0)])  10.8 us
  transfers between devices with their start and end apart: 1, of which 1 were waited for; matrix products, arithmetic and copies ran while one was open for 0% of the time, Pallas kernels for 0%

profile of v3, /device:TPU:1, one launch (start us, length us, event | category | flops | bytes accessed | tf_op | source)
XLA Modules:
  0.0 110.8 jit_solution(858914729318704596)
XLA Ops:
  0.6 1.8 %shard_map.86 = bf16[32,88,128]{2,1,0:T(8,128)(2,1)S(1)} custom-call(bf16[1024,128]{1,0:T(8,128)(2,1)} %x_hbm.1, bf16[128,128]{1,0:T(8,128)(2,1)} %bi_hbm.1, bf16[128,512]{1,0:T(8,128)(2,1)} %ql_hbm.1, bf16[448,512]{1,0:T(8,128)(2,1)} %bo_ref.1, bf16[448,512]{1,0:T(8,128)(2,1)} %qr_hbm.1), custom_call_target="tpu_custom_call" | custom-call | tf_op jit(solution)/shard_map/pallas_call | solution.py:147
  2.4 0.0 copy-start.2
  2.4 30.3 %all_to_all.25.r_ref = bf16[32,88,128]{2,1,0:T(8,128)(2,1)S(1)} all-to-all(bf16[32,88,128]{2,1,0:T(8,128)(2,1)S(1)} %shard_map.86), channel_id=1, replica_groups=mesh['dp'=8,'zh'=2,'y'=8,'x'=4] {'y','x'}, dimensions={0} | all-to-all | bytes 1441792 | tf_op jit(solution)/shard_map/all_to_all | solution.py:161
  32.7 0.0 copy-start.1
  32.7 0.0 copy-done.2
  32.7 0.1 shard_map.87.a_ref
  32.8 0.0 copy-start
  32.9 10.8 %collective-permute-start = (f32[56,128]{1,0:T(8,128)S(1)}, f32[56,128]{1,0:T(8,128)S(1)}, u32[]{:S(2)}, u32[]{:S(2)}) collective-permute-start(f32[56,128]{1,0:T(8,128)S(1)} %shard_map.87.a_ref), channel_id=1, source_target_pairs={{0,32},{32,0},{1,33},{33,1},{2,34},{34,2},{3,35},{35,3},{4,36},{36... | collective-permute-start | bytes 86024 | tf_op jit(solution)/shard_map/ppermute | solution.py:163
  43.6 1.3 %collective-permute-done.b_ref = f32[56,128]{1,0:T(8,128)S(1)} collective-permute-done((f32[56,128]{1,0:T(8,128)S(1)}, f32[56,128]{1,0:T(8,128)S(1)}, u32[]{:S(2)}, u32[]{:S(2)}) %collective-permute-start) | collective-permute-done | bytes 28704 | tf_op jit(solution)/shard_map/ppermute | solution.py:163
  44.9 16.1 %all_to_all.26.r_ref = bf16[32,40,128]{2,1,0:T(8,128)(2,1)S(1)} all-to-all(bf16[32,40,128]{2,1,0:T(8,128)(2,1)S(1)} %get-tuple-element.13), channel_id=1, replica_groups=mesh['dp'=8,'zh'=2,'y'=8,'x'=4] {'y','x'}, dimensions={0} | all-to-all | bytes 655360 | tf_op jit(solution)/shard_map/all_to_all | solution.py:166
  61.1 0.0 copy-done.1
  61.1 0.0 copy-done
  61.1 1.2 %shard_map.89 = (f32[32,16,128]{2,1,0:T(8,128)S(1)}, f32[32,128]{1,0:T(8,128)S(1)}) custom-call(bf16[32,40,128]{2,1,0:T(8,128)(2,1)S(1)} %all_to_all.26.r_ref, bf16[448,1024]{1,0:T(8,128)(2,1)S(1)} %bitcast.5, bf16[448,512]{1,0:T(8,128)(2,1)S(1)} %copy-done, f32[8,128]{1,0:T(8,128)S(1)} %get-tuple-element.14.right_ref), custom_call_target="tpu_custom_call" | custom-call | tf_op jit(solution)/shard_map/pallas_call | solution.py:22
  62.3 14.3 %all_to_all.27.r_ref = f32[32,16,128]{2,1,0:T(8,128)S(1)} all-to-all(f32[32,16,128]{2,1,0:T(8,128)S(1)} %get-tuple-element.15), channel_id=1, replica_groups=mesh['dp'=8,'zh'=2,'y'=8,'x'=4] {'y','x'}, dimensions={0} | all-to-all | bytes 524288 | tf_op jit(solution)/shard_map/all_to_all | solution.py:169
  76.7 21.2 %all_to_all.28.r_ref = f32[16,16,128]{2,1,0:T(8,128)S(1)} all-to-all(f32[16,16,128]{2,1,0:T(8,128)S(1)} %get-tuple-element.17), channel_id=1, replica_groups=mesh['dp'=8,'zh'=2,'y'=8,'x'=4] {'dp','zh'}, dimensions={0} | all-to-all | bytes 262144 | tf_op jit(solution)/shard_map/all_to_all | solution.py:171
  97.9 0.2 shard_map.91
  98.0 12.1 %all_to_all.29.r_ref = f32[32,1,128]{2,1,0:T(1,128)S(1)} all-to-all(f32[32,1,128]{2,1,0:T(1,128)S(1)} %get-tuple-element.20), channel_id=1, replica_groups=mesh['dp'=8,'zh'=2,'y'=8,'x'=4] {'y','x'}, dimensions={0} | all-to-all | bytes 32768 | tf_op jit(solution)/shard_map/all_to_all | solution.py:173
  110.2 0.6 shard_map.92
  (2 shorter events, 0.1 us)
Async XLA Ops:
  2.4 30.3 %copy-start.2 = (f32[128,8]{0,1:T(8,128)S(1)}, f32[128,8]{0,1:T(8,128)}, u32[]{:S(2)}) copy-start(f32[128,8]{0,1:T(8,128)} %param.13) | copy-start | bytes 12292
  32.7 28.3 %copy-start.1 = (bf16[1024,448]{0,1:T(8,128)(2,1)S(1)}, bf16[1024,448]{0,1:T(8,128)(2,1)}, u32[]{:S(2)}) copy-start(bf16[1024,448]{0,1:T(8,128)(2,1)} %param.8) | copy-start | bytes 2752516
  32.8 28.2 %copy-start = (bf16[448,512]{1,0:T(8,128)(2,1)S(1)}, bf16[448,512]{1,0:T(8,128)(2,1)}, u32[]{:S(2)}) copy-start(bf16[448,512]{1,0:T(8,128)(2,1)} %bo_ref.1) | copy-start | bytes 1376260
  32.9 12.0 %collective-permute-start = (f32[56,128]{1,0:T(8,128)S(1)}, f32[56,128]{1,0:T(8,128)S(1)}, u32[]{:S(2)}, u32[]{:S(2)}) collective-permute-start(f32[56,128]{1,0:T(8,128)S(1)} %shard_map.87.a_ref), channel_id=1, source_target_pairs={{0,32},{32,0},{1,33},{33,1},{2,34},{34,2},{3,35},{35,3},{4,36},{36... | collective-permute-start | bytes 86024 | tf_op jit(solution)/shard_map/ppermute | solution.py:163

commit v4 on v3

--- a/solution.py
+++ b/solution.py
@@ -12,6 +12,8 @@
 PLANE = ("y", "x")
 COLUMN = ("dp", "zh")
 N = 32
+LOW = 16
+TAIL = 32 + LOW
 
 
 def tn(a, b):
@@ -39,7 +41,9 @@
         (bi_hbm, bi_ref), (x_hbm, x_ref), (ql_hbm.at[:, block], ql_ref),
         (qr_hbm.at[:, block], qr_ref), (bo_hbm.at[:, half], bo_ref),
     ]
-    moves = [pltpu.make_async_copy(src, dst, sem.at[k]) for k, (src, dst) in enumerate(moves)]
+    moves = [
+        pltpu.make_async_copy(src, dst, sem.at[k]) for k, (src, dst) in enumerate(moves)
+    ]
     for move in moves:
         move.start()
     moves[0].wait()
@@ -47,7 +51,7 @@
     proj = jnp.dot(x_ref[...], bi_ref[...], preferred_element_type=F32)
     high, low = split(proj)
     o_ref[:, 0:32, :] = high.astype(BF16).reshape(N, 32, 128)
-    o_ref[:, 32:64, :] = low.astype(BF16).reshape(N, 32, 128)
+    o_ref[:, 32:TAIL, :] = low.astype(BF16).reshape(N, 32, 128)[:, 0:LOW]
     moves[2].wait()
     high, low = split(tn(ql_ref[...], bi_ref[...]).reshape(N // 2, 8, 128))
     top = lax.broadcasted_iota(jnp.int32, (N // 2, 8, 128), 1) < 4
@@ -57,14 +61,16 @@
     moves[3].wait()
     moves[4].wait()
     high, low = split(tn(bo_ref[...], qr_ref[...]).reshape(N, 8, 128))
-    o_ref[:, 64:88, :] = jnp.concatenate([high, low, left], axis=1).astype(BF16)
+    o_ref[:, TAIL : TAIL + 24, :] = jnp.concatenate([high, low, left], axis=1).astype(BF16)
 
 
 def plane_sum(r_ref, eig_ref, o_ref):
     total = jnp.sum(r_ref[...].astype(F32), axis=0)
-    o_ref[0:32] = total[0:32] + total[32:64]
-    o_ref[32:40] = total[64:72] + total[72:80]
-    o_ref[40:48] = total[80:88]
+    rest = total[TAIL:]
+    o_ref[0:LOW] = total[0:LOW] + total[32:TAIL]
+    o_ref[LOW:32] = total[LOW:32]
+    o_ref[32:40] = rest[0:8] + rest[8:16]
+    o_ref[40:48] = rest[16:24]
     o_ref[48:56] = eig_ref[...]
 
 
@@ -146,7 +152,7 @@
     hbm = pl.BlockSpec(memory_space=pltpu.HBM)
     part = pl.pallas_call(
         partials,
-        out_shape=shape(N, 88, 128, dtype=BF16),
+        out_shape=shape(N, TAIL + 24, 128, dtype=BF16),
         in_specs=[hbm] * 5,
         scratch_shapes=[
             pltpu.VMEM((1024, 128), BF16),

time: 111 us -> 109 us (0.982)
  blocking collectives: 94.1 us -> 91.5 us
    all_to_all x1, blocking collectives: 30.3 us -> 28 us  [on_device(): part = lax.all_to_all(part, PLANE, 0, 0, tiled=True)]
where the time goes in v4:
time: 109 us; the launch traced here: 108 us
  blocking collectives  91.5 us (84%)
  starting transfers between devices  10.8 us (10%)
  Pallas kernels  3.95 us (4%)
  waiting for transfers between devices  1.27 us (1%)
    all_to_all x1, blocking collectives, on_device(): part = lax.all_to_all(part, PLANE, 0, 0, tiled=True)  28 us
    all_to_all x1, blocking collectives, on_device(): packed = lax.all_to_all(packed, COLUMN, 0, 0, tiled=True)  20.7 us
    all_to_all x1, blocking collectives, on_device(): full = lax.all_to_all(full, PLANE, 0, 0, tiled=True)  16 us
    all_to_all x1, blocking collectives, on_device(): rotated = lax.all_to_all(rotated, PLANE, 0, 0, tiled=True)  14.8 us
    all_to_all x1, blocking collectives, on_device(): scores = lax.all_to_all(scores, PLANE, 0, 0, tiled=True)  12.1 us
    ppermute x1, starting transfers between devices, on_device(): other = lax.ppermute(mine, 'zh', [(0, 1), (1, 0)])  10.8 us
  transfers between devices with their start and end apart: 1, of which 1 were waited for; matrix products, arithmetic and copies ran while one was open for 0% of the time, Pallas kernels for 0%

profile of v4, /device:TPU:1, one launch (start us, length us, event | category | flops | bytes accessed | tf_op | source)
XLA Modules:
  0.0 108.3 jit_solution(496870803913293378)
XLA Ops:
  0.6 1.8 %shard_map.86 = bf16[32,72,128]{2,1,0:T(8,128)(2,1)S(1)} custom-call(bf16[1024,128]{1,0:T(8,128)(2,1)} %x_hbm.1, bf16[128,128]{1,0:T(8,128)(2,1)} %bi_hbm.1, bf16[128,512]{1,0:T(8,128)(2,1)} %ql_hbm.1, bf16[448,512]{1,0:T(8,128)(2,1)} %bo_ref.1, bf16[448,512]{1,0:T(8,128)(2,1)} %qr_hbm.1), custom_call_target="tpu_custom_call" | custom-call | tf_op jit(solution)/shard_map/pallas_call | solution.py:153
  2.4 0.0 copy-start.2
  2.4 0.0 copy-start.1
  2.4 28.0 %all_to_all.25.r_ref = bf16[32,72,128]{2,1,0:T(8,128)(2,1)S(1)} all-to-all(bf16[32,72,128]{2,1,0:T(8,128)(2,1)S(1)} %shard_map.86), channel_id=1, replica_groups=mesh['dp'=8,'zh'=2,'y'=8,'x'=4] {'y','x'}, dimensions={0} | all-to-all | bytes 1179648 | tf_op jit(solution)/shard_map/all_to_all | solution.py:167
  30.4 0.0 copy-done.2
  30.4 0.1 shard_map.87.a_ref
  30.5 0.0 copy-start
  30.5 10.8 %collective-permute-start = (f32[56,128]{1,0:T(8,128)S(1)}, f32[56,128]{1,0:T(8,128)S(1)}, u32[]{:S(2)}, u32[]{:S(2)}) collective-permute-start(f32[56,128]{1,0:T(8,128)S(1)} %shard_map.87.a_ref), channel_id=1, source_target_pairs={{0,32},{32,0},{1,33},{33,1},{2,34},{34,2},{3,35},{35,3},{4,36},{36... | collective-permute-start | bytes 86024 | tf_op jit(solution)/shard_map/ppermute | solution.py:169
  41.3 1.3 %collective-permute-done.b_ref = f32[56,128]{1,0:T(8,128)S(1)} collective-permute-done((f32[56,128]{1,0:T(8,128)S(1)}, f32[56,128]{1,0:T(8,128)S(1)}, u32[]{:S(2)}, u32[]{:S(2)}) %collective-permute-start) | collective-permute-done | bytes 28704 | tf_op jit(solution)/shard_map/ppermute | solution.py:169
  42.6 16.0 %all_to_all.26.r_ref = bf16[32,40,128]{2,1,0:T(8,128)(2,1)S(1)} all-to-all(bf16[32,40,128]{2,1,0:T(8,128)(2,1)S(1)} %get-tuple-element.13), channel_id=1, replica_groups=mesh['dp'=8,'zh'=2,'y'=8,'x'=4] {'y','x'}, dimensions={0} | all-to-all | bytes 655360 | tf_op jit(solution)/shard_map/all_to_all | solution.py:172
  58.6 0.0 copy-done.1
  58.6 0.0 copy-done
  58.6 1.2 %shard_map.89 = (f32[32,16,128]{2,1,0:T(8,128)S(1)}, f32[32,128]{1,0:T(8,128)S(1)}) custom-call(bf16[32,40,128]{2,1,0:T(8,128)(2,1)S(1)} %all_to_all.26.r_ref, bf16[448,1024]{1,0:T(8,128)(2,1)S(1)} %bitcast.5, bf16[448,512]{1,0:T(8,128)(2,1)S(1)} %copy-done, f32[8,128]{1,0:T(8,128)S(1)} %get-tuple-element.14.right_ref), custom_call_target="tpu_custom_call" | custom-call | tf_op jit(solution)/shard_map/pallas_call | solution.py:24
  59.9 14.8 %all_to_all.27.r_ref = f32[32,16,128]{2,1,0:T(8,128)S(1)} all-to-all(f32[32,16,128]{2,1,0:T(8,128)S(1)} %get-tuple-element.15), channel_id=1, replica_groups=mesh['dp'=8,'zh'=2,'y'=8,'x'=4] {'y','x'}, dimensions={0} | all-to-all | bytes 524288 | tf_op jit(solution)/shard_map/all_to_all | solution.py:175
  74.7 20.7 %all_to_all.28.r_ref = f32[16,16,128]{2,1,0:T(8,128)S(1)} all-to-all(f32[16,16,128]{2,1,0:T(8,128)S(1)} %get-tuple-element.17), channel_id=1, replica_groups=mesh['dp'=8,'zh'=2,'y'=8,'x'=4] {'dp','zh'}, dimensions={0} | all-to-all | bytes 262144 | tf_op jit(solution)/shard_map/all_to_all | solution.py:177
  95.4 0.2 shard_map.91
  95.6 12.1 %all_to_all.29.r_ref = f32[32,1,128]{2,1,0:T(1,128)S(1)} all-to-all(f32[32,1,128]{2,1,0:T(1,128)S(1)} %get-tuple-element.20), channel_id=1, replica_groups=mesh['dp'=8,'zh'=2,'y'=8,'x'=4] {'y','x'}, dimensions={0} | all-to-all | bytes 32768 | tf_op jit(solution)/shard_map/all_to_all | solution.py:179
  107.7 0.6 shard_map.92
  (2 shorter events, 0.1 us)
Async XLA Ops:
  2.4 28.0 %copy-start.2 = (f32[128,8]{0,1:T(8,128)S(1)}, f32[128,8]{0,1:T(8,128)}, u32[]{:S(2)}) copy-start(f32[128,8]{0,1:T(8,128)} %param.13) | copy-start | bytes 12292
  2.4 56.2 %copy-start.1 = (bf16[1024,448]{0,1:T(8,128)(2,1)S(1)}, bf16[1024,448]{0,1:T(8,128)(2,1)}, u32[]{:S(2)}) copy-start(bf16[1024,448]{0,1:T(8,128)(2,1)} %param.8) | copy-start | bytes 2752516
  30.5 28.1 %copy-start = (bf16[448,512]{1,0:T(8,128)(2,1)S(1)}, bf16[448,512]{1,0:T(8,128)(2,1)}, u32[]{:S(2)}) copy-start(bf16[448,512]{1,0:T(8,128)(2,1)} %bo_ref.1) | copy-start | bytes 1376260
  30.5 12.1 %collective-permute-start = (f32[56,128]{1,0:T(8,128)S(1)}, f32[56,128]{1,0:T(8,128)S(1)}, u32[]{:S(2)}, u32[]{:S(2)}) collective-permute-start(f32[56,128]{1,0:T(8,128)S(1)} %shard_map.87.a_ref), channel_id=1, source_target_pairs={{0,32},{32,0},{1,33},{33,1},{2,34},{34,2},{3,35},{35,3},{4,36},{36... | collective-permute-start | bytes 86024 | tf_op jit(solution)/shard_map/ppermute | solution.py:169

commit v5 on v4

--- a/solution.py
+++ b/solution.py
@@ -90,10 +90,8 @@
 def rotate(r_ref, g_ref, bo_ref, right_ref, o_ref, w_ref):
     proj = r_ref[:, 0:32, :].reshape(N * 32, 128)
     moment = jnp.dot(g_ref[...], proj, preferred_element_type=F32)
-    m1, rest = split(moment)
-    m2, m3 = split(rest)
-    rotated = tn(bo_ref[...], jnp.concatenate([m1, m2, m3], axis=1).astype(BF16))
-    rotated = (rotated[:, 256:384] + rotated[:, 128:256]) + rotated[:, 0:128]
+    rotated = tn(bo_ref[...], jnp.concatenate(split(moment), axis=1).astype(BF16))
+    rotated = rotated[:, 128:256] + rotated[:, 0:128]
     o_ref[:, 0:8, :] = rotated[0:256].reshape(N, 8, 128)
     o_ref[:, 8:16, :] = rotated[256:512].reshape(N, 8, 128)
     pieces = r_ref[:, 32:40, :].astype(F32)

time: 109 us -> 108 us (level)
  no operation moved by 1% of the time
where the time goes in v5:
time: 108 us
  blocking collectives  91.5 us (85%)
  starting transfers between devices  10.8 us (10%)
  Pallas kernels  3.71 us (3%)
  waiting for transfers between devices  1.27 us (1%)
    all_to_all x1, blocking collectives, on_device(): part = lax.all_to_all(part, PLANE, 0, 0, tiled=True)  28 us
    all_to_all x1, blocking collectives, on_device(): packed = lax.all_to_all(packed, COLUMN, 0, 0, tiled=True)  20.7 us
    all_to_all x1, blocking collectives, on_device(): full = lax.all_to_all(full, PLANE, 0, 0, tiled=True)  16 us
    all_to_all x1, blocking collectives, on_device(): rotated = lax.all_to_all(rotated, PLANE, 0, 0, tiled=True)  14.8 us
    all_to_all x1, blocking collectives, on_device(): scores = lax.all_to_all(scores, PLANE, 0, 0, tiled=True)  12.1 us
    ppermute x1, starting transfers between devices, on_device(): other = lax.ppermute(mine, 'zh', [(0, 1), (1, 0)])  10.8 us
  transfers between devices with their start and end apart: 1, of which 1 were waited for; matrix products, arithmetic and copies ran while one was open for 0% of the time, Pallas kernels for 0%

profile of v5, /device:TPU:1, one launch (start us, length us, event | category | flops | bytes accessed | tf_op | source)
XLA Modules:
  0.0 108.0 jit_solution(10364655230230272483)
XLA Ops:
  0.6 1.8 %shard_map.86 = bf16[32,72,128]{2,1,0:T(8,128)(2,1)S(1)} custom-call(bf16[1024,128]{1,0:T(8,128)(2,1)} %x_hbm.1, bf16[128,128]{1,0:T(8,128)(2,1)} %bi_hbm.1, bf16[128,512]{1,0:T(8,128)(2,1)} %ql_hbm.1, bf16[448,512]{1,0:T(8,128)(2,1)} %bo_ref.1, bf16[448,512]{1,0:T(8,128)(2,1)} %qr_hbm.1), custom_call_target="tpu_custom_call" | custom-call | tf_op jit(solution)/shard_map/pallas_call | solution.py:151
  2.4 0.0 copy-start.2
  2.4 0.0 copy-start.1
  2.4 28.0 %all_to_all.25.r_ref = bf16[32,72,128]{2,1,0:T(8,128)(2,1)S(1)} all-to-all(bf16[32,72,128]{2,1,0:T(8,128)(2,1)S(1)} %shard_map.86), channel_id=1, replica_groups=mesh['dp'=8,'zh'=2,'y'=8,'x'=4] {'y','x'}, dimensions={0} | all-to-all | bytes 1179648 | tf_op jit(solution)/shard_map/all_to_all | solution.py:165
  30.4 0.0 copy-done.2
  30.4 0.1 shard_map.87.a_ref
  30.5 0.0 copy-start
  30.5 10.8 %collective-permute-start = (f32[56,128]{1,0:T(8,128)S(1)}, f32[56,128]{1,0:T(8,128)S(1)}, u32[]{:S(2)}, u32[]{:S(2)}) collective-permute-start(f32[56,128]{1,0:T(8,128)S(1)} %shard_map.87.a_ref), channel_id=1, source_target_pairs={{0,32},{32,0},{1,33},{33,1},{2,34},{34,2},{3,35},{35,3},{4,36},{36... | collective-permute-start | bytes 86024 | tf_op jit(solution)/shard_map/ppermute | solution.py:167
  41.3 1.3 %collective-permute-done.b_ref = f32[56,128]{1,0:T(8,128)S(1)} collective-permute-done((f32[56,128]{1,0:T(8,128)S(1)}, f32[56,128]{1,0:T(8,128)S(1)}, u32[]{:S(2)}, u32[]{:S(2)}) %collective-permute-start) | collective-permute-done | bytes 28704 | tf_op jit(solution)/shard_map/ppermute | solution.py:167
  42.6 16.0 %all_to_all.26.r_ref = bf16[32,40,128]{2,1,0:T(8,128)(2,1)S(1)} all-to-all(bf16[32,40,128]{2,1,0:T(8,128)(2,1)S(1)} %get-tuple-element.13), channel_id=1, replica_groups=mesh['dp'=8,'zh'=2,'y'=8,'x'=4] {'y','x'}, dimensions={0} | all-to-all | bytes 655360 | tf_op jit(solution)/shard_map/all_to_all | solution.py:170
  58.6 0.0 copy-done.1
  58.6 0.0 copy-done
  58.6 1.0 shard_map.89
  59.6 14.8 %all_to_all.27.r_ref = f32[32,16,128]{2,1,0:T(8,128)S(1)} all-to-all(f32[32,16,128]{2,1,0:T(8,128)S(1)} %get-tuple-element.15), channel_id=1, replica_groups=mesh['dp'=8,'zh'=2,'y'=8,'x'=4] {'y','x'}, dimensions={0} | all-to-all | bytes 524288 | tf_op jit(solution)/shard_map/all_to_all | solution.py:173
  74.5 20.7 %all_to_all.28.r_ref = f32[16,16,128]{2,1,0:T(8,128)S(1)} all-to-all(f32[16,16,128]{2,1,0:T(8,128)S(1)} %get-tuple-element.17), channel_id=1, replica_groups=mesh['dp'=8,'zh'=2,'y'=8,'x'=4] {'dp','zh'}, dimensions={0} | all-to-all | bytes 262144 | tf_op jit(solution)/shard_map/all_to_all | solution.py:175
  95.2 0.2 shard_map.91
  95.3 12.1 %all_to_all.29.r_ref = f32[32,1,128]{2,1,0:T(1,128)S(1)} all-to-all(f32[32,1,128]{2,1,0:T(1,128)S(1)} %get-tuple-element.20), channel_id=1, replica_groups=mesh['dp'=8,'zh'=2,'y'=8,'x'=4] {'y','x'}, dimensions={0} | all-to-all | bytes 32768 | tf_op jit(solution)/shard_map/all_to_all | solution.py:177
  107.4 0.6 shard_map.92
  (2 shorter events, 0.1 us)
Async XLA Ops:
  2.4 28.0 %copy-start.2 = (f32[128,8]{0,1:T(8,128)S(1)}, f32[128,8]{0,1:T(8,128)}, u32[]{:S(2)}) copy-start(f32[128,8]{0,1:T(8,128)} %param.13) | copy-start | bytes 12292
  2.4 56.2 %copy-start.1 = (bf16[1024,448]{0,1:T(8,128)(2,1)S(1)}, bf16[1024,448]{0,1:T(8,128)(2,1)}, u32[]{:S(2)}) copy-start(bf16[1024,448]{0,1:T(8,128)(2,1)} %param.8) | copy-start | bytes 2752516
  30.5 28.1 %copy-start = (bf16[448,512]{1,0:T(8,128)(2,1)S(1)}, bf16[448,512]{1,0:T(8,128)(2,1)}, u32[]{:S(2)}) copy-start(bf16[448,512]{1,0:T(8,128)(2,1)} %bo_ref.1) | copy-start | bytes 1376260
  30.5 12.1 %collective-permute-start = (f32[56,128]{1,0:T(8,128)S(1)}, f32[56,128]{1,0:T(8,128)S(1)}, u32[]{:S(2)}, u32[]{:S(2)}) collective-permute-start(f32[56,128]{1,0:T(8,128)S(1)} %shard_map.87.a_ref), channel_id=1, source_target_pairs={{0,32},{32,0},{1,33},{33,1},{2,34},{34,2},{3,35},{35,3},{4,36},{36... | collective-permute-start | bytes 86024 | tf_op jit(solution)/shard_map/ppermute | solution.py:167

commit v6 on v5

--- a/solution.py
+++ b/solution.py
@@ -46,20 +46,17 @@
     ]
     for move in moves:
         move.start()
-    moves[0].wait()
-    moves[1].wait()
+    for move in moves:
+        move.wait()
     proj = jnp.dot(x_ref[...], bi_ref[...], preferred_element_type=F32)
     high, low = split(proj)
     o_ref[:, 0:32, :] = high.astype(BF16).reshape(N, 32, 128)
     o_ref[:, 32:TAIL, :] = low.astype(BF16).reshape(N, 32, 128)[:, 0:LOW]
-    moves[2].wait()
     high, low = split(tn(ql_ref[...], bi_ref[...]).reshape(N // 2, 8, 128))
     top = lax.broadcasted_iota(jnp.int32, (N // 2, 8, 128), 1) < 4
     even = jnp.where(top, high, jnp.roll(low, 4, axis=1))
     odd = jnp.where(top, jnp.roll(high, 4, axis=1), low)
     left = jnp.concatenate([even[:, None], odd[:, None]], axis=1).reshape(N, 8, 128)
-    moves[3].wait()
-    moves[4].wait()
     high, low = split(tn(bo_ref[...], qr_ref[...]).reshape(N, 8, 128))
     o_ref[:, TAIL : TAIL + 24, :] = jnp.concatenate([high, low, left], axis=1).astype(BF16)
 

time: 108 us -> 108 us (level)
  no operation moved by 1% of the time
where the time goes in v6:
time: 108 us
  blocking collectives  91.6 us (85%)
  starting transfers between devices  10.8 us (10%)
  Pallas kernels  3.41 us (3%)
  waiting for transfers between devices  1.27 us (1%)
    all_to_all x1, blocking collectives, on_device(): part = lax.all_to_all(part, PLANE, 0, 0, tiled=True)  28 us
    all_to_all x1, blocking collectives, on_device(): packed = lax.all_to_all(packed, COLUMN, 0, 0, tiled=True)  20.7 us
    all_to_all x1, blocking collectives, on_device(): full = lax.all_to_all(full, PLANE, 0, 0, tiled=True)  16 us
    all_to_all x1, blocking collectives, on_device(): rotated = lax.all_to_all(rotated, PLANE, 0, 0, tiled=True)  14.8 us
    all_to_all x1, blocking collectives, on_device(): scores = lax.all_to_all(scores, PLANE, 0, 0, tiled=True)  12.1 us
    ppermute x1, starting transfers between devices, on_device(): other = lax.ppermute(mine, 'zh', [(0, 1), (1, 0)])  10.8 us
  transfers between devices with their start and end apart: 1, of which 1 were waited for; matrix products, arithmetic and copies ran while one was open for 0% of the time, Pallas kernels for 0%

profile of v6, /device:TPU:1, one launch (start us, length us, event | category | flops | bytes accessed | tf_op | source)
XLA Modules:
  0.0 107.7 jit_solution(11367474898162918833)
XLA Ops:
  0.6 1.5 %shard_map.86 = bf16[32,72,128]{2,1,0:T(8,128)(2,1)S(1)} custom-call(bf16[1024,128]{1,0:T(8,128)(2,1)} %x_hbm.1, bf16[128,128]{1,0:T(8,128)(2,1)} %bi_hbm.1, bf16[128,512]{1,0:T(8,128)(2,1)} %ql_hbm.1, bf16[448,512]{1,0:T(8,128)(2,1)} %bo_ref.1, bf16[448,512]{1,0:T(8,128)(2,1)} %qr_hbm.1), custom_call_target="tpu_custom_call" | custom-call | tf_op jit(solution)/shard_map/pallas_call | solution.py:148
  2.1 0.0 copy-start.2
  2.1 0.0 copy-start.1
  2.1 28.0 %all_to_all.25.r_ref = bf16[32,72,128]{2,1,0:T(8,128)(2,1)S(1)} all-to-all(bf16[32,72,128]{2,1,0:T(8,128)(2,1)S(1)} %shard_map.86), channel_id=1, replica_groups=mesh['dp'=8,'zh'=2,'y'=8,'x'=4] {'y','x'}, dimensions={0} | all-to-all | bytes 1179648 | tf_op jit(solution)/shard_map/all_to_all | solution.py:162
  30.1 0.0 copy-done.2
  30.1 0.1 shard_map.87.a_ref
  30.2 0.0 copy-start
  30.3 10.8 %collective-permute-start = (f32[56,128]{1,0:T(8,128)S(1)}, f32[56,128]{1,0:T(8,128)S(1)}, u32[]{:S(2)}, u32[]{:S(2)}) collective-permute-start(f32[56,128]{1,0:T(8,128)S(1)} %shard_map.87.a_ref), channel_id=1, source_target_pairs={{0,32},{32,0},{1,33},{33,1},{2,34},{34,2},{3,35},{35,3},{4,36},{36... | collective-permute-start | bytes 86024 | tf_op jit(solution)/shard_map/ppermute | solution.py:164
  41.0 1.3 %collective-permute-done.b_ref = f32[56,128]{1,0:T(8,128)S(1)} collective-permute-done((f32[56,128]{1,0:T(8,128)S(1)}, f32[56,128]{1,0:T(8,128)S(1)}, u32[]{:S(2)}, u32[]{:S(2)}) %collective-permute-start) | collective-permute-done | bytes 28704 | tf_op jit(solution)/shard_map/ppermute | solution.py:164
  42.3 16.0 %all_to_all.26.r_ref = bf16[32,40,128]{2,1,0:T(8,128)(2,1)S(1)} all-to-all(bf16[32,40,128]{2,1,0:T(8,128)(2,1)S(1)} %get-tuple-element.13), channel_id=1, replica_groups=mesh['dp'=8,'zh'=2,'y'=8,'x'=4] {'y','x'}, dimensions={0} | all-to-all | bytes 655360 | tf_op jit(solution)/shard_map/all_to_all | solution.py:167
  58.3 0.0 copy-done.1
  58.3 0.0 copy-done
  58.3 1.0 shard_map.89
  59.3 14.8 %all_to_all.27.r_ref = f32[32,16,128]{2,1,0:T(8,128)S(1)} all-to-all(f32[32,16,128]{2,1,0:T(8,128)S(1)} %get-tuple-element.15), channel_id=1, replica_groups=mesh['dp'=8,'zh'=2,'y'=8,'x'=4] {'y','x'}, dimensions={0} | all-to-all | bytes 524288 | tf_op jit(solution)/shard_map/all_to_all | solution.py:170
  74.2 20.7 %all_to_all.28.r_ref = f32[16,16,128]{2,1,0:T(8,128)S(1)} all-to-all(f32[16,16,128]{2,1,0:T(8,128)S(1)} %get-tuple-element.17), channel_id=1, replica_groups=mesh['dp'=8,'zh'=2,'y'=8,'x'=4] {'dp','zh'}, dimensions={0} | all-to-all | bytes 262144 | tf_op jit(solution)/shard_map/all_to_all | solution.py:172
  94.9 0.2 shard_map.91
  95.0 12.1 %all_to_all.29.r_ref = f32[32,1,128]{2,1,0:T(1,128)S(1)} all-to-all(f32[32,1,128]{2,1,0:T(1,128)S(1)} %get-tuple-element.20), channel_id=1, replica_groups=mesh['dp'=8,'zh'=2,'y'=8,'x'=4] {'y','x'}, dimensions={0} | all-to-all | bytes 32768 | tf_op jit(solution)/shard_map/all_to_all | solution.py:174
  107.1 0.6 shard_map.92
  (2 shorter events, 0.1 us)
Async XLA Ops:
  2.1 28.0 %copy-start.2 = (f32[128,8]{0,1:T(8,128)S(1)}, f32[128,8]{0,1:T(8,128)}, u32[]{:S(2)}) copy-start(f32[128,8]{0,1:T(8,128)} %param.13) | copy-start | bytes 12292
  2.1 56.2 %copy-start.1 = (bf16[1024,448]{0,1:T(8,128)(2,1)S(1)}, bf16[1024,448]{0,1:T(8,128)(2,1)}, u32[]{:S(2)}) copy-start(bf16[1024,448]{0,1:T(8,128)(2,1)} %param.8) | copy-start | bytes 2752516
  30.2 28.1 %copy-start = (bf16[448,512]{1,0:T(8,128)(2,1)S(1)}, bf16[448,512]{1,0:T(8,128)(2,1)}, u32[]{:S(2)}) copy-start(bf16[448,512]{1,0:T(8,128)(2,1)} %bo_ref.1) | copy-start | bytes 1376260
  30.3 12.0 %collective-permute-start = (f32[56,128]{1,0:T(8,128)S(1)}, f32[56,128]{1,0:T(8,128)S(1)}, u32[]{:S(2)}, u32[]{:S(2)}) collective-permute-start(f32[56,128]{1,0:T(8,128)S(1)} %shard_map.87.a_ref), channel_id=1, source_target_pairs={{0,32},{32,0},{1,33},{33,1},{2,34},{34,2},{3,35},{35,3},{4,36},{36... | collective-permute-start | bytes 86024 | tf_op jit(solution)/shard_map/ppermute | solution.py:164

commit v7 on v6

--- a/solution.py
+++ b/solution.py
@@ -100,7 +100,11 @@
     query = lax.broadcasted_iota(jnp.int32, (32, 128), 0) // 8
     column = lax.broadcasted_iota(jnp.int32, (32, 128), 1) // 32
     rows = jnp.where(query == column, rows, 0.0)
-    w_ref[...] = jnp.dot(rows, left, precision=lax.Precision.HIGHEST, preferred_element_type=F32)
+    r1, r2 = split(rows)
+    l1, l2 = split(left)
+    rows = jnp.concatenate([r1, r1, r2], axis=1).astype(BF16)
+    left = jnp.concatenate([l1, l2, l1], axis=0).astype(BF16)
+    w_ref[...] = jnp.dot(rows, left, preferred_element_type=F32)
 
 
 def column_pack(r_ref, w_ref, o_ref, s_ref):

time: 108 us -> 108 us (level)
  no operation moved by 1% of the time
where the time goes in v7:
time: 108 us
  blocking collectives  91.6 us (85%)
  starting transfers between devices  10.8 us (10%)
  Pallas kernels  3.39 us (3%)
  waiting for transfers between devices  1.27 us (1%)
    all_to_all x1, blocking collectives, on_device(): part = lax.all_to_all(part, PLANE, 0, 0, tiled=True)  28 us
    all_to_all x1, blocking collectives, on_device(): packed = lax.all_to_all(packed, COLUMN, 0, 0, tiled=True)  20.7 us
    all_to_all x1, blocking collectives, on_device(): full = lax.all_to_all(full, PLANE, 0, 0, tiled=True)  16 us
    all_to_all x1, blocking collectives, on_device(): rotated = lax.all_to_all(rotated, PLANE, 0, 0, tiled=True)  14.8 us
    all_to_all x1, blocking collectives, on_device(): scores = lax.all_to_all(scores, PLANE, 0, 0, tiled=True)  12.1 us
    ppermute x1, starting transfers between devices, on_device(): other = lax.ppermute(mine, 'zh', [(0, 1), (1, 0)])  10.8 us
  transfers between devices with their start and end apart: 1, of which 1 were waited for; matrix products, arithmetic and copies ran while one was open for 0% of the time, Pallas kernels for 0%

profile of v7, /device:TPU:1, one launch (start us, length us, event | category | flops | bytes accessed | tf_op | source)
XLA Modules:
  0.0 107.7 jit_solution(15122813590233428426)
XLA Ops:
  0.6 1.5 %shard_map.86 = bf16[32,72,128]{2,1,0:T(8,128)(2,1)S(1)} custom-call(bf16[1024,128]{1,0:T(8,128)(2,1)} %x_hbm.1, bf16[128,128]{1,0:T(8,128)(2,1)} %bi_hbm.1, bf16[128,512]{1,0:T(8,128)(2,1)} %ql_hbm.1, bf16[448,512]{1,0:T(8,128)(2,1)} %bo_ref.1, bf16[448,512]{1,0:T(8,128)(2,1)} %qr_hbm.1), custom_call_target="tpu_custom_call" | custom-call | tf_op jit(solution)/shard_map/pallas_call | solution.py:152
  2.1 0.0 copy-start.2
  2.1 0.0 copy-start.1
  2.1 28.0 %all_to_all.25.r_ref = bf16[32,72,128]{2,1,0:T(8,128)(2,1)S(1)} all-to-all(bf16[32,72,128]{2,1,0:T(8,128)(2,1)S(1)} %shard_map.86), channel_id=1, replica_groups=mesh['dp'=8,'zh'=2,'y'=8,'x'=4] {'y','x'}, dimensions={0} | all-to-all | bytes 1179648 | tf_op jit(solution)/shard_map/all_to_all | solution.py:166
  30.1 0.0 copy-done.2
  30.1 0.1 shard_map.87.a_ref
  30.2 0.0 copy-start
  30.3 10.8 %collective-permute-start = (f32[56,128]{1,0:T(8,128)S(1)}, f32[56,128]{1,0:T(8,128)S(1)}, u32[]{:S(2)}, u32[]{:S(2)}) collective-permute-start(f32[56,128]{1,0:T(8,128)S(1)} %shard_map.87.a_ref), channel_id=1, source_target_pairs={{0,32},{32,0},{1,33},{33,1},{2,34},{34,2},{3,35},{35,3},{4,36},{36... | collective-permute-start | bytes 86024 | tf_op jit(solution)/shard_map/ppermute | solution.py:168
  41.0 1.3 %collective-permute-done.b_ref = f32[56,128]{1,0:T(8,128)S(1)} collective-permute-done((f32[56,128]{1,0:T(8,128)S(1)}, f32[56,128]{1,0:T(8,128)S(1)}, u32[]{:S(2)}, u32[]{:S(2)}) %collective-permute-start) | collective-permute-done | bytes 28704 | tf_op jit(solution)/shard_map/ppermute | solution.py:168
  42.3 16.0 %all_to_all.26.r_ref = bf16[32,40,128]{2,1,0:T(8,128)(2,1)S(1)} all-to-all(bf16[32,40,128]{2,1,0:T(8,128)(2,1)S(1)} %get-tuple-element.13), channel_id=1, replica_groups=mesh['dp'=8,'zh'=2,'y'=8,'x'=4] {'y','x'}, dimensions={0} | all-to-all | bytes 655360 | tf_op jit(solution)/shard_map/all_to_all | solution.py:171
  58.3 0.0 copy-done.1
  58.3 0.0 copy-done
  58.3 1.0 shard_map.89
  59.3 14.8 %all_to_all.27.r_ref = f32[32,16,128]{2,1,0:T(8,128)S(1)} all-to-all(f32[32,16,128]{2,1,0:T(8,128)S(1)} %get-tuple-element.15), channel_id=1, replica_groups=mesh['dp'=8,'zh'=2,'y'=8,'x'=4] {'y','x'}, dimensions={0} | all-to-all | bytes 524288 | tf_op jit(solution)/shard_map/all_to_all | solution.py:174
  74.2 20.7 %all_to_all.28.r_ref = f32[16,16,128]{2,1,0:T(8,128)S(1)} all-to-all(f32[16,16,128]{2,1,0:T(8,128)S(1)} %get-tuple-element.17), channel_id=1, replica_groups=mesh['dp'=8,'zh'=2,'y'=8,'x'=4] {'dp','zh'}, dimensions={0} | all-to-all | bytes 262144 | tf_op jit(solution)/shard_map/all_to_all | solution.py:176
  94.8 0.2 shard_map.91
  95.0 12.1 %all_to_all.29.r_ref = f32[32,1,128]{2,1,0:T(1,128)S(1)} all-to-all(f32[32,1,128]{2,1,0:T(1,128)S(1)} %get-tuple-element.20), channel_id=1, replica_groups=mesh['dp'=8,'zh'=2,'y'=8,'x'=4] {'y','x'}, dimensions={0} | all-to-all | bytes 32768 | tf_op jit(solution)/shard_map/all_to_all | solution.py:178
  107.1 0.6 shard_map.92
  (2 shorter events, 0.1 us)
Async XLA Ops:
  2.1 28.0 %copy-start.2 = (f32[128,8]{0,1:T(8,128)S(1)}, f32[128,8]{0,1:T(8,128)}, u32[]{:S(2)}) copy-start(f32[128,8]{0,1:T(8,128)} %param.13) | copy-start | bytes 12292
  2.1 56.2 %copy-start.1 = (bf16[1024,448]{0,1:T(8,128)(2,1)S(1)}, bf16[1024,448]{0,1:T(8,128)(2,1)}, u32[]{:S(2)}) copy-start(bf16[1024,448]{0,1:T(8,128)(2,1)} %param.8) | copy-start | bytes 2752516
  30.2 28.1 %copy-start = (bf16[448,512]{1,0:T(8,128)(2,1)S(1)}, bf16[448,512]{1,0:T(8,128)(2,1)}, u32[]{:S(2)}) copy-start(bf16[448,512]{1,0:T(8,128)(2,1)} %bo_ref.1) | copy-start | bytes 1376260
  30.3 12.0 %collective-permute-start = (f32[56,128]{1,0:T(8,128)S(1)}, f32[56,128]{1,0:T(8,128)S(1)}, u32[]{:S(2)}, u32[]{:S(2)}) collective-permute-start(f32[56,128]{1,0:T(8,128)S(1)} %shard_map.87.a_ref), channel_id=1, source_target_pairs={{0,32},{32,0},{1,33},{33,1},{2,34},{34,2},{3,35},{35,3},{4,36},{36... | collective-permute-start | bytes 86024 | tf_op jit(solution)/shard_map/ppermute | solution.py:168
